TPU v7x, 128 devices: a whole 4x4x4 slice. The times are simulated.
128 devices in a mesh: lat: 16 (over x, y), var: 8 (over z, core).
Axes of the slice: x: 4, y: 4, z: 4, core: 2. Of those that a mesh axis runs over, the one named last changes fastest.
Arguments:
- patches: bfloat16 [96, 192, 1024], P('lat', 'var'), may hold values from -6 to 6
- norm_gain: float32 [1024], replicated, may hold values from 0.25 to 1.75
- input_proj: bfloat16 [1024, 3072], replicated, may hold values from -7 to 7
- output_proj: bfloat16 [1024, 1024], replicated, may hold values from -0.1875 to 0.1875
- level_scale: float32 [40, 1024], P('var'), may hold values from 0.1 to 1.9
- level_shift: float32 [40, 1024], P('var'), may hold values from -3 to 3
- head_weight: bfloat16 [40, 1024, 320], P('var', 'lat'), may hold values from -0.1875 to 0.1875
- targets: bfloat16 [40, 96, 192, 320], P('var', 'lat'), may hold values from -6 to 6
- level_counts: int32 [4], replicated, may hold values from 13 to 37
- tile_dataset: int32 [16, 8], P('lat'), may hold values from 0 to 3
- slot_level: int32 [40], P('var'), may hold values from 0 to 39, as said below
Outputs:
- latent: bfloat16 [96, 192, 1024], P('lat', 'var')
- grad_latent: bfloat16 [96, 192, 1024], P('lat', 'var')
- grad_head: float32 [40, 1024, 320], P('var', 'lat')
Inputs may be any that keep to these rules, and one draw needn't show every extreme that they name: `slot_level`: for each j, slots j * 5 to (j + 1) * 5 - 1 hold the levels j * 5 to (j + 1) * 5 - 1 in some order.
All inputs are finite; a program needn't handle non-finite values.
Results may differ from a plain program's by a relative error of at most 0.012.
Values may be sent and summed in bfloat16 or wider, within the bound.
A program may use at most 128 MiB of HBM per device.

v0:
```python
import math
import jax
import jax.numpy as jnp
from jax import lax
from jax.sharding import PartitionSpec as P

HEADS = 16
WH = 6
WW = 12
EPS = 1e-05


def padded(array, sides, width, wrap):
    for axis, dim in sides:
        size, length = (lax.axis_size(axis), array.shape[dim])
        up = [(i, (i + 1) % size) for i in range(size if wrap else size - 1)]
        down = [(j, i) for i, j in up]
        last = lax.slice_in_dim(array, length - width, length, axis=dim)
        initial = lax.slice_in_dim(array, 0, width, axis=dim)
        before = lax.ppermute(last, axis, up)
        after = lax.ppermute(initial, axis, down)
        array = jnp.concatenate([before, array, after], axis=dim)
    return array


def layer_norm(values, gain):
    wide = values.astype(jnp.float32)
    average = jnp.mean(wide, axis=-1, keepdims=True)
    centred = wide - average
    variance = jnp.mean(centred * centred, axis=-1, keepdims=True)
    return (centred * lax.rsqrt(variance + EPS) * gain).astype(jnp.bfloat16)


def window_attention(query_ext, keyval, row_valid, heads):
    ext_rows, ext_cols, width = query_ext.shape
    head_size = width // heads
    win_rows = ext_rows // WH
    win_cols = ext_cols // WW

    def split(values, parts):
        shaped = values.reshape(win_rows, WH, win_cols, WW, parts, heads, head_size)
        return shaped.transpose(0, 2, 1, 3, 4, 5, 6).reshape(
            win_rows * win_cols, WH * WW, parts, heads, head_size
        )

    query_win = split(query_ext, 1)[:, :, 0]
    pairs = split(keyval, 2)
    key_win = pairs[:, :, 0]
    value_win = pairs[:, :, 1]
    key_mask = jnp.broadcast_to(
        row_valid.reshape(win_rows, 1, WH, 1), (win_rows, win_cols, WH, WW)
    ).reshape(win_rows * win_cols, WH * WW)
    scores = jnp.einsum(
        "wqhd,wkhd->whqk", query_win, key_win, preferred_element_type=jnp.float32
    ) / math.sqrt(head_size)
    scores = jnp.where(key_mask[:, None, None, :], scores, -jnp.inf)
    peak = jnp.max(scores, axis=-1, keepdims=True)
    weights = jnp.exp(scores - peak)
    probs = (weights / jnp.sum(weights, axis=-1, keepdims=True)).astype(jnp.bfloat16)
    mixed = jnp.einsum("whqk,wkhd->wqhd", probs, value_win, preferred_element_type=jnp.float32)
    return (
        mixed.reshape(win_rows, win_cols, WH, WW, width)
        .transpose(0, 2, 1, 3, 4)
        .reshape(ext_rows, ext_cols, width)
    )


def slot_terms(piece, target_rows, live_cols, level_scale, level_shift, heads_full):
    piece_wide = piece.astype(jnp.float32)
    rows = (
        piece_wide[None] * level_scale[:, None, None, :] + level_shift[:, None, None, :]
    ).astype(jnp.bfloat16)
    predicted = jnp.einsum("krnd,kdo->krno", rows, heads_full, preferred_element_type=jnp.float32)
    errors = ((predicted - target_rows.astype(jnp.float32)) * live_cols[:, None, :, None]).astype(
        jnp.bfloat16
    )
    back_grad = jnp.einsum("krno,kdo->krnd", errors, heads_full, preferred_element_type=jnp.float32)
    piece_grad = jnp.sum(back_grad * level_scale[:, None, None, :], axis=0)
    head_add = jnp.einsum("krnd,krno->dko", rows, errors, preferred_element_type=jnp.float32)
    return (piece_grad, head_add)


def local(
    patches,
    norm_gain,
    input_proj,
    output_proj,
    level_scale,
    level_shift,
    head_weight,
    targets,
    level_counts,
    tile_dataset,
    slot_level,
):
    band_rows, band_cols, width = patches.shape
    half_rows = WH // 2
    half_cols = WW // 2
    lat_count = lax.axis_size("lat")
    var_count = lax.axis_size("var")
    lat_place = lax.axis_index("lat")
    ext_rows = band_rows + WH
    ext_cols = band_cols + WW
    extended = padded(patches, (("lat", 0),), half_rows, False)
    extended = padded(extended, (("var", 1),), half_cols, True)
    normed_ext = layer_norm(extended, norm_gain)
    keyval = jnp.dot(
        normed_ext.reshape(-1, width), input_proj[:, width:], preferred_element_type=jnp.float32
    )
    keyval = keyval.astype(jnp.bfloat16).reshape(ext_rows, ext_cols, 2 * width)
    normed = normed_ext[half_rows : half_rows + band_rows, half_cols : half_cols + band_cols]
    queries = jnp.dot(
        normed.reshape(-1, width), input_proj[:, :width], preferred_element_type=jnp.float32
    )
    queries = queries.astype(jnp.bfloat16).reshape(band_rows, band_cols, width)
    query_ext = jnp.pad(queries, ((half_rows, WH - half_rows), (half_cols, WW - half_cols), (0, 0)))
    global_row = lat_place * band_rows - half_rows + jnp.arange(ext_rows, dtype=jnp.int32)
    row_valid = (global_row >= 0) & (global_row < lat_count * band_rows)
    mixed = window_attention(query_ext, keyval, row_valid, HEADS)
    attn = mixed[half_rows : half_rows + band_rows, half_cols : half_cols + band_cols].astype(
        jnp.bfloat16
    )
    update = jnp.dot(
        attn.reshape(-1, width), output_proj, preferred_element_type=jnp.float32
    ).reshape(band_rows, band_cols, width)
    latent = (patches.astype(jnp.float32) + update).astype(jnp.bfloat16)
    dataset_row = tile_dataset[0]
    dataset_ids = jnp.arange(level_counts.shape[0], dtype=jnp.int32)
    tile_levels = jnp.sum(
        jnp.where(dataset_row[:, None] == dataset_ids[None, :], level_counts[None, :], 0), axis=1
    )
    live_tiles = (slot_level[None, :] < tile_levels[:, None]).astype(jnp.float32)
    heads_full = lax.all_gather(head_weight, "lat", axis=1, tiled=True)
    tile_ids = jnp.arange(var_count, dtype=jnp.int32)
    piece = lax.all_gather(latent, "var", axis=1, tiled=True)
    piece_cols = piece.shape[1]
    column_tile = jnp.arange(piece_cols, dtype=jnp.int32) // band_cols
    onehot = (column_tile[:, None] == tile_ids[None, :]).astype(jnp.float32)
    column_live = jnp.dot(onehot, live_tiles)
    piece_grad, head_add = slot_terms(
        piece, targets, column_live.T, level_scale, level_shift, heads_full
    )
    latent_terms = piece_grad
    latent_terms, head_terms = (latent_terms, head_add)
    grad_latent = lax.psum_scatter(
        latent_terms.astype(jnp.bfloat16), "var", scatter_dimension=1, tiled=True
    )
    head_terms = head_terms * (1.0 / math.sqrt(lat_count * band_rows * var_count * band_cols))
    share_rows = width // lat_count
    mine = lax.psum_scatter(
        head_terms.astype(jnp.bfloat16), "lat", scatter_dimension=0, tiled=True
    ).astype(jnp.float32)
    grad_head = jnp.transpose(mine, (1, 0, 2))
    return (latent, grad_latent, grad_head)


def solution(mesh):
    in_specs = (
        P("lat", "var", None),
        P(),
        P(),
        P(),
        P("var", None),
        P("var", None),
        P("var", "lat", None),
        P("var", "lat", None, None),
        P(),
        P("lat", None),
        P("var"),
    )
    out_specs = (P("lat", "var", None), P("lat", "var", None), P("var", "lat", None))
    return jax.shard_map(local, mesh=mesh, in_specs=in_specs, out_specs=out_specs, check_vma=False)
```

profile of v0, /device:TPU:0, one launch (start us, length us, event | category | flops | bytes accessed | tf_op | source)
XLA Modules:
  0.0 313.8 jit_solution(12802649083848093492)
XLA Ops:
  8.4 3.6 %collective-permute-start = (bf16[3,24,1024]{2,1,0:T(8,128)(2,1)S(1)}, bf16[3,24,1024]{2,1,0:T(8,128)(2,1)S(1)}, u32[]{:S(2)}, u32[]{:S(2)}) collective-permute-start(bf16[3,24,1024]{2,1,0:T(8,128)(2,1)S(1)} %get-tuple-element.25), channel_id=1, source_target_pairs={{0,8},{8,16},{16,24},{24,32},{32,40},{40,48},{48,56},{56,64},{64,7... | collective-permute-start | bytes 442376 | tf_op jit(solution)/shard_map/ppermute | solution.py:20
  13.3 1.8 collective-permute-done
  16.0 3.1 collective-permute-done.1
  19.3 2.9 collective-permute-start.3
  22.4 3.2 %collective-permute-done.2 = bf16[12,6,1024]{2,1,0:T(8,128)(2,1)S(1)} collective-permute-done((bf16[12,6,1024]{2,1,0:T(8,128)(2,1)S(1)}, bf16[12,6,1024]{2,1,0:T(8,128)(2,1)S(1)}, u32[]{:S(2)}, u32[]{:S(2)}) %collective-permute-start.2) | collective-permute-done | bytes 147488 | tf_op jit(solution)/shard_map/ppermute | solution.py:20
  26.1 1.8 multiply_reduce_fusion.1
  29.7 2.7 reshape.102
  33.7 2.1 fusion.40
  35.9 2.1 reshape.99
  38.0 3.2 %copy.48 = bf16[2,3,6,12,1,16,64]{6,5,3,2,1,0,4:T(8,128)(2,1)} copy(bf16[2,3,6,12,1,16,64]{6,5,3,1,2,0,4:T(8,128)(2,1)} %bitcast.58) | data formatting | bytes 1769472 | tf_op jit(solution)/shard_map/transpose | solution.py:42
  41.2 5.5 %fusion.15 = bf16[432,2048]{1,0:T(8,128)(2,1)} fusion(bf16[1024,3072]{1,0:T(8,128)(2,1)} %param.13, f32[432,1024]{1,0:T(8,128)S(1)} %copy-done.2, f32[1024]{0:T(1024)S(1)} %copy-done.4, f32[432]{0:T(512)S(1)} %rsqrt.13, f32[432]{0:T(512)S(1)} %div.33), kind=kOutput, calls=%fused_computation.22 | convolution fusion | flops 1814593536 | bytes 7740800 | tf_op jit(solution)/shard_map/dot_general | solution.py:107
  46.8 6.4 %reshape_reshape.3 = bf16[2,6,3,12,2,16,64]{6,5,4,3,2,1,0:T(8,128)(2,1)} reshape(bf16[432,2048]{1,0:T(8,128)(2,1)} %fusion.15) | data formatting | bytes 3538944 | tf_op jit(solution)/shard_map/reshape;reshape | solution.py:41
  53.1 2.6 copy.46
  55.7 2.6 fusion.59
  58.3 4.0 %copy.61 = bf16[6,72,1,16,64]{1,4,3,0,2:T(8,128)(2,1)} copy(bf16[6,72,1,16,64]{4,3,2,1,0:T(8,128)(2,1)} %get-tuple-element.18) | data formatting | bytes 1769472
  62.4 4.0 %copy.62 = bf16[6,72,1,16,64]{1,4,3,0,2:T(8,128)(2,1)} copy(bf16[6,72,1,16,64]{4,3,2,1,0:T(8,128)(2,1)} %get-tuple-element.19) | data formatting | bytes 1769472
  66.4 3.1 fusion.25
  69.5 1.8 fusion.62
  71.3 1.9 fusion.34
  73.2 4.0 %copy.52 = bf16[6,72,16,64]{3,2,1,0:T(8,128)(2,1)} copy(bf16[6,72,16,64]{1,3,2,0:T(8,128)(2,1)} %fusion.34) | data formatting | bytes 1769472 | tf_op jit(solution)/shard_map/whqk,wkhd->wqhd/transpose | solution.py:60
  77.2 3.9 %reshape.100 = bf16[2,3,6,12,1024]{4,3,2,1,0:T(8,128)(2,1)} reshape(bf16[6,72,16,64]{3,2,1,0:T(8,128)(2,1)} %copy.52) | data formatting | bytes 1769472 | tf_op jit(solution)/shard_map/reshape | solution.py:62
  83.6 2.3 fusion.43
  87.1 28.5 %all-gather.3.cloned.1.call-done = bf16[6,192,1024]{2,1,0:T(8,128)(2,1)} async-done(((bf16[6,24,1024]{2,1,0:T(8,128)(2,1)}), bf16[6,192,1024]{2,1,0:T(8,128)(2,1)}) %all-gather.3.cloned.1.call-update) | async-done | bytes 2359312 | tf_op jit(solution)/shard_map/all_gather | solution.py:135
  115.6 4.3 %convert_element_type.67 = f32[6,192,1024]{2,1,0:T(8,128)} convert(bf16[6,192,1024]{2,1,0:T(8,128)(2,1)} %all-gather.3.cloned.1.call-done) | non-fusion elementwise | flops 1179648 | bytes 7077888 | tf_op jit(solution)/shard_map/convert_element_type | solution.py:69
  119.9 48.6 %all-gather.5.cloned.1.call-done = bf16[5,1024,320]{2,1,0:T(8,128)(2,1)} async-done(((bf16[5,64,320]{2,1,0:T(8,128)(2,1)}), bf16[5,1024,320]{2,1,0:T(8,128)(2,1)}) %all-gather.5.cloned.1.call-update) | async-done | bytes 3276816 | tf_op jit(solution)/shard_map/all_gather | solution.py:133
  168.5 10.6 %multiply_convert_fusion = bf16[5,6,192,320]{3,2,1,0:T(8,128)(2,1)S(1)} fusion(bf16[5,6,192,320]{3,2,1,0:T(8,128)(2,1)} %param.18, f32[5,192]{1,0:T(8,128)S(1)} %fusion.52, bf16[5,1024,320]{2,1,0:T(8,128)(2,1)} %all-gather.5.cloned.1.call-done, f32[5,1024]{1,0:T(8,128)S(1)} %copy-done.7, f32[5,1024]{1,0:T(8,128)S(1)} %copy-done.6, ...), kind=kOutput, calls=%fused_computation.11 | convolution fusion | flops 3799941120 | bytes 15412992 | tf_op jit(solution)/shard_map/krnd,kdo->krno/dot_general | solution.py:73
  179.2 7.2 %multiply_reduce_fusion = bf16[6,192,1024]{2,1,0:T(8,128)(2,1)S(1)} fusion(f32[5,1024]{1,0:T(8,128)S(1)} %copy-done.6, bf16[5,6,192,320]{3,2,1,0:T(8,128)(2,1)S(1)} %multiply_convert_fusion, bf16[5,1024,320]{2,1,0:T(8,128)(2,1)S(1)} %copy-done.5), kind=kOutput, calls=%fused_computation.1 | convolution fusion | flops 3785490432 | bytes 9342976 | tf_op jit(solution)/shard_map/krno,kdo->krnd/dot_general | solution.py:77
  186.4 1.7 copy.63
  188.2 9.3 %fusion.14 = bf16[1024,5,320]{0,2,1:T(8,128)(2,1)} fusion(bf16[5,6,192,320]{3,2,1,0:T(8,128)(2,1)} %copy-done.11, f32[5,1024]{1,0:T(8,128)S(1)} %copy-done.7, f32[5,1024]{1,0:T(8,128)S(1)} %copy-done.6, f32[6,192,1024]{2,1,0:T(8,128)} %convert_element_type.67), kind=kOutput, calls=%fused_computation.21 | convolution fusion | flops 3795845120 | bytes 11722752 | tf_op jit(solution)/shard_map/krnd,krno->dko/dot_general | solution.py:79
  197.5 8.2 %copy.54 = bf16[1024,5,320]{2,1,0:T(8,128)(2,1)} copy(bf16[1024,5,320]{0,2,1:T(8,128)(2,1)} %fusion.14) | data formatting | bytes 6553600 | tf_op jit(solution)/shard_map/convert_element_type | solution.py:151
  205.7 16.5 %reduce-scatter.7.cloned.1.call-done = bf16[24,6144]{1,0:T(8,128)(2,1)} async-done(((bf16[192,6144]{1,0:T(8,128)(2,1)}), bf16[24,6144]{1,0:T(8,128)(2,1)}) %reduce-scatter.7.cloned.1.call-update) | async-done | bytes 294928
  224.4 80.9 %reduce-scatter.5.cloned.1.call-done = bf16[64,5,320]{2,1,0:T(8,128)(2,1)} async-done(((bf16[1024,5,320]{2,1,0:T(8,128)(2,1)}), bf16[64,5,320]{2,1,0:T(8,128)(2,1)}) %reduce-scatter.5.cloned.1.call-update) | async-done | bytes 204816 | tf_op jit(solution)/shard_map/reduce_scatter | solution.py:150
  (61 shorter events, 15.3 us)
Async XLA Ops:
  7.2 76.4 %copy-start = (bf16[1024,1024]{1,0:T(8,128)(2,1)S(1)}, bf16[1024,1024]{1,0:T(8,128)(2,1)}, u32[]{:S(2)}) copy-start(bf16[1024,1024]{1,0:T(8,128)(2,1)} %param.14) | copy-start | bytes 6291460
  7.2 108.4 %all-gather.3.cloned.1.call-start = ((), (), s32[]{:S(2)}) async-start(), calls=%async_computation.2 | async-start | bytes 2654208 | tf_op jit(solution)/shard_map/all_gather | solution.py:135
  8.4 6.7 %collective-permute-start = (bf16[3,24,1024]{2,1,0:T(8,128)(2,1)S(1)}, bf16[3,24,1024]{2,1,0:T(8,128)(2,1)S(1)}, u32[]{:S(2)}, u32[]{:S(2)}) collective-permute-start(bf16[3,24,1024]{2,1,0:T(8,128)(2,1)S(1)} %get-tuple-element.25), channel_id=1, source_target_pairs={{0,8},{8,16},{16,24},{24,32},{32,40},{40,48},{48,56},{56,64},{64,7... | collective-permute-start | bytes 442376 | tf_op jit(solution)/shard_map/ppermute | solution.py:20
  12.0 7.2 %collective-permute-start.1 = (bf16[3,24,1024]{2,1,0:T(8,128)(2,1)S(1)}, bf16[3,24,1024]{2,1,0:T(8,128)(2,1)S(1)}, u32[]{:S(2)}, u32[]{:S(2)}) collective-permute-start(bf16[3,24,1024]{2,1,0:T(8,128)(2,1)S(1)} %get-tuple-element.24), channel_id=1, source_target_pairs={{8,0},{16,8},{24,16},{32,24},{40,32},{48,40},{56,48},{64,56},{72,6... | collective-permute-start | bytes 442376 | tf_op jit(solution)/shard_map/ppermute | solution.py:21
  19.2 6.3 %collective-permute-start.2 = (bf16[12,6,1024]{2,1,0:T(8,128)(2,1)S(1)}, bf16[12,6,1024]{2,1,0:T(8,128)(2,1)S(1)}, u32[]{:S(2)}, u32[]{:S(2)}) collective-permute-start(bf16[12,6,1024]{2,1,0:T(8,128)(2,1)S(1)} %get-tuple-element.22), channel_id=1, source_target_pairs={{0,1},{1,2},{2,3},{3,4},{4,5},{5,6},{6,7},{7,0},{8,9},{9,10},{10,1... | collective-permute-start | bytes 442376 | tf_op jit(solution)/shard_map/ppermute | solution.py:20
  19.3 6.3 %collective-permute-start.3 = (bf16[12,6,1024]{2,1,0:T(8,128)(2,1)S(1)}, bf16[12,6,1024]{2,1,0:T(8,128)(2,1)S(1)}, u32[]{:S(2)}, u32[]{:S(2)}) collective-permute-start(bf16[12,6,1024]{2,1,0:T(8,128)(2,1)S(1)} %get-tuple-element.23), channel_id=1, source_target_pairs={{1,0},{2,1},{3,2},{4,3},{5,4},{6,5},{7,6},{0,7},{9,8},{10,9},{11,1... | collective-permute-start | bytes 442376 | tf_op jit(solution)/shard_map/ppermute | solution.py:21
  27.9 4.5 %copy-start.4 = (f32[1024]{0:T(1024)S(1)}, f32[1024]{0:T(1024)}, u32[]{:S(2)}) copy-start(f32[1024]{0:T(1024)} %param.12) | copy-start | bytes 12292
  38.0 3.2 %copy-start.2 = (f32[432,1024]{1,0:T(8,128)S(1)}, f32[432,1024]{1,0:T(8,128)}, u32[]{:S(2)}) copy-start(f32[432,1024]{1,0:T(8,128)} %reshape.102) | copy-start | bytes 5308420
  69.5 1.8 copy-start.3
  82.5 4.2 %copy-start.8 = (s32[4]{0:T(128)S(1)}, s32[4]{0:T(128)}, u32[]{:S(2)}) copy-start(s32[4]{0:T(128)} %param.19) | copy-start | bytes 52
  82.5 4.2 %copy-start.9 = (s32[1,8]{1,0:T(1,128)S(1)}, s32[1,8]{1,0:T(1,128)}, u32[]{:S(2)}) copy-start(s32[1,8]{1,0:T(1,128)} %param.20) | copy-start | bytes 100
  82.5 4.3 %copy-start.10 = (s32[5]{0:T(128)S(1)}, s32[5]{0:T(128)}, u32[]{:S(2)}) copy-start(s32[5]{0:T(128)} %param.21) | copy-start | bytes 64
  85.9 82.6 %all-gather.5.cloned.1.call-start = ((), (), s32[]{:S(2)}) async-start(), calls=%async_computation.3 | async-start | bytes 4177920 | tf_op jit(solution)/shard_map/all_gather | solution.py:133
  86.6 135.5 %reduce-scatter.7.cloned.1.call-start = ((), (), s32[]{:S(2)}) async-start(), calls=%async_computation.5 | async-start | bytes 2654208
  87.1 81.5 %copy-start.6 = (f32[5,1024]{1,0:T(8,128)S(1)}, f32[5,1024]{1,0:T(8,128)}, u32[]{:S(2)}) copy-start(f32[5,1024]{1,0:T(8,128)} %param.15) | copy-start | bytes 61444
  87.1 81.5 %copy-start.7 = (f32[5,1024]{1,0:T(8,128)S(1)}, f32[5,1024]{1,0:T(8,128)}, u32[]{:S(2)}) copy-start(f32[5,1024]{1,0:T(8,128)} %param.16) | copy-start | bytes 61444
  168.5 10.6 %copy-start.5 = (bf16[5,1024,320]{2,1,0:T(8,128)(2,1)S(1)}, bf16[5,1024,320]{2,1,0:T(8,128)(2,1)}, u32[]{:S(2)}) copy-start(bf16[5,1024,320]{2,1,0:T(8,128)(2,1)} %all-gather.5.cloned.1.call-done) | copy-start | bytes 9830404
  179.2 7.2 %copy-start.11 = (bf16[5,6,192,320]{3,2,1,0:T(8,128)(2,1)}, bf16[5,6,192,320]{3,2,1,0:T(8,128)(2,1)S(1)}, u32[]{:S(2)}) copy-start(bf16[5,6,192,320]{3,2,1,0:T(8,128)(2,1)S(1)} %multiply_convert_fusion) | copy-start | bytes 11059204
  188.1 117.2 %reduce-scatter.5.cloned.1.call-start = ((), (), s32[]{:S(2)}) async-start(), calls=%async_computation.4 | async-start | bytes 6684672 | tf_op jit(solution)/shard_map/reduce_scatter | solution.py:150
  205.7 101.6 %copy-start.1 = (bf16[1024,1024]{1,0:T(8,128)(2,1)S(1)}, bf16[1024,1024]{1,0:T(8,128)(2,1)}, u32[]{:S(2)}) copy-start(bf16[1024,1024]{1,0:T(8,128)(2,1)} %param.14) | copy-start | bytes 6291460
Sparse Core Ops, SparseCore 0:
  86.0 29.4 all-gather.2
  117.7 50.7 all-gather.4
  188.2 33.9 reduce-scatter.6
  225.5 79.7 reduce-scatter.4
where the time goes:
time: 315 us; the launch traced here: 314 us
  waiting for transfers between devices  183 us (58%)
  local copies, waits for them, and re-layouts  53.8 us (17%)
  matrix products  42.2 us (13%)
  between operations  14 us (4%)
  other arithmetic  12.5 us (4%)
  starting transfers between devices  7.98 us (3%)
    reduce_scatter x1, waiting for transfers between devices, local(): lax.psum_scatter(head_terms.astype(jnp.bfloat16), 'lat', scatter_dimensio...  80.9 us
    all_gather x1, waiting for transfers between devices, local(): heads_full = lax.all_gather(head_weight, 'lat', axis=1, tiled=True)  48.6 us
    all_gather x1, waiting for transfers between devices, local(): piece = lax.all_gather(latent, 'var', axis=1, tiled=True)  28.5 us
    unnamed x5, waiting for transfers between devices  17.3 us
    unnamed x32, local copies, waits for them, and re-layouts  13.9 us
    dot_general x1, matrix products, slot_terms(): jnp.einsum('krnd,kdo->krno', rows, heads_full, preferred_element_type=jnp...  10.6 us
    dot_general x1, matrix products, slot_terms(): jnp.einsum('krnd,krno->dko', rows, errors, preferred_element_type=jnp.flo...  9.29 us
    another operation x2, local copies, waits for them, and re-layouts, split(): shaped = values.reshape(win_rows, WH, win_cols, WW, parts, heads, head_size)  8.98 us
  transfers between devices with their start and end apart: 8, of which 7 were waited for; matrix products, arithmetic and copies ran while one was open for 8% of the time, Pallas kernels for 0%

commit v1 on v0

--- a/solution.py
+++ b/solution.py
@@ -8,6 +8,22 @@
 WH = 6
 WW = 12
 EPS = 1e-05
+
+
+def _switch_layers_all(arr_in):
+    world = lax.axis_size("lat")
+    lanes = [(hop_no, (hop_no + 1) % world) for hop_no in range(world)]
+    samples = [(hop_no, (hop_no - 1) % world) for hop_no in range(world)]
+    odd, h_now = ([arr_in], [arr_in])
+    for _ in range(world // 2):
+        arr_now = lax.ppermute(odd[-1], "lat", lanes)
+        odd.append(arr_now)
+    for _ in range((world - 1) // 2):
+        mid_arr = lax.ppermute(h_now[-1], "lat", samples)
+        h_now.append(mid_arr)
+    z1 = jnp.concatenate([*odd[::-1], *h_now[1:]], axis=1)
+    f_next = lax.axis_index("lat")
+    return jnp.roll(z1, shift=(f_next - world // 2) * arr_in.shape[1], axis=1)
 
 
 def padded(array, sides, width, wrap):
@@ -130,7 +146,7 @@
         jnp.where(dataset_row[:, None] == dataset_ids[None, :], level_counts[None, :], 0), axis=1
     )
     live_tiles = (slot_level[None, :] < tile_levels[:, None]).astype(jnp.float32)
-    heads_full = lax.all_gather(head_weight, "lat", axis=1, tiled=True)
+    heads_full = _switch_layers_all(head_weight)
     tile_ids = jnp.arange(var_count, dtype=jnp.int32)
     piece = lax.all_gather(latent, "var", axis=1, tiled=True)
     piece_cols = piece.shape[1]

time: 315 us -> 356 us (1.13)
  starting transfers between devices: 7.98 us -> 45.4 us
  local copies, waits for them, and re-layouts: 53.8 us -> 72.6 us
  waiting for transfers between devices: 183 us -> 168 us
    ppermute x0 -> x15, waiting for transfers between devices: none -> 63.5 us  [the longest x8 63.5 us: _switch_layers_all(): arr_now = lax.ppermute(odd[-1], 'lat', lanes)]
    all_gather x1 -> x0, waiting for transfers between devices: 48.6 us -> none  [local(): heads_full = lax.all_gather(head_weight, 'lat', axis=1, tiled=True)]
    ppermute x0 -> x15, starting transfers between devices: none -> 37.5 us  [the longest x7 35.8 us: _switch_layers_all(): mid_arr = lax.ppermute(h_now[-1], 'lat', samples)]
    all_gather x1, waiting for transfers between devices: 28.5 us -> 0.02 us  [local(): piece = lax.all_gather(latent, 'var', axis=1, tiled=True)]
    concatenate x0 -> x1, local copies, waits for them, and re-layouts: none -> 15.2 us  [_switch_layers_all(): return jnp.roll(z1, shift=(f_next - world // 2) * arr_in.shape[1], axis=1)]
    unnamed x32 -> x43, local copies, waits for them, and re-layouts: 13.9 us -> 17.4 us
    unnamed x5 -> x4, waiting for transfers between devices: 17.3 us -> 15.6 us
  transfers between devices with their start and end apart: 8 -> 22, of which waited for: 7 -> 13; matrix products, arithmetic and copies ran while one was open for 8% -> 10% of each run, Pallas kernels for 0% -> 0%
where the time goes in v1:
time: 356 us; the launch traced here: 353 us
  waiting for transfers between devices  168 us (47%)
  local copies, waits for them, and re-layouts  72.6 us (20%)
  starting transfers between devices  45.4 us (13%)
  matrix products  42.6 us (12%)
  between operations  14.1 us (4%)
  other arithmetic  10.5 us (3%)
    reduce_scatter x1, waiting for transfers between devices, local(): lax.psum_scatter(head_terms.astype(jnp.bfloat16), 'lat', scatter_dimensio...  81.1 us
    ppermute x8, waiting for transfers between devices, _switch_layers_all(): arr_now = lax.ppermute(odd[-1], 'lat', lanes)  63.5 us
    ppermute x7, starting transfers between devices, _switch_layers_all(): mid_arr = lax.ppermute(h_now[-1], 'lat', samples)  35.8 us
    unnamed x43, local copies, waits for them, and re-layouts  17.4 us
    unnamed x4, waiting for transfers between devices  15.6 us
    concatenate x1, local copies, waits for them, and re-layouts, _switch_layers_all(): return jnp.roll(z1, shift=(f_next - world // 2) * arr_in.shape[1], axis=1)  15.2 us
    dot_general x1, matrix products, slot_terms(): jnp.einsum('krnd,kdo->krno', rows, heads_full, preferred_element_type=jnp...  10.9 us
    dot_general x1, matrix products, slot_terms(): jnp.einsum('krnd,krno->dko', rows, errors, preferred_element_type=jnp.flo...  9.27 us
  transfers between devices with their start and end apart: 22, of which 13 were waited for; matrix products, arithmetic and copies ran while one was open for 10% of the time, Pallas kernels for 0%

profile of v1, /device:TPU:0, one launch (start us, length us, event | category | flops | bytes accessed | tf_op | source)
XLA Modules:
  0.0 353.5 jit_solution(9327504747094295079)
XLA Ops:
  8.4 3.6 %collective-permute-start = (bf16[3,24,1024]{2,1,0:T(8,128)(2,1)S(1)}, bf16[3,24,1024]{2,1,0:T(8,128)(2,1)S(1)}, u32[]{:S(2)}, u32[]{:S(2)}) collective-permute-start(bf16[3,24,1024]{2,1,0:T(8,128)(2,1)S(1)} %get-tuple-element.25), channel_id=1, source_target_pairs={{0,8},{8,16},{16,24},{24,32},{32,40},{40,48},{48,56},{56,64},{64,7... | collective-permute-start | bytes 442376 | tf_op jit(solution)/shard_map/ppermute | solution.py:36
  16.0 3.1 collective-permute-done.1
  22.4 3.2 collective-permute-done.2
  38.1 3.2 copy.64
  41.3 5.5 %fusion.17 = bf16[432,2048]{1,0:T(8,128)(2,1)} fusion(bf16[1024,3072]{1,0:T(8,128)(2,1)} %param.13, f32[432,1024]{1,0:T(8,128)S(1)} %copy-done.4, f32[1024]{0:T(1024)S(1)} %copy-done.10, f32[432]{0:T(512)S(1)} %rsqrt.13, f32[432]{0:T(512)S(1)} %div.33), kind=kOutput, calls=%fused_computation.24 | convolution fusion | flops 1814593536 | bytes 7740800 | tf_op jit(solution)/shard_map/dot_general | solution.py:123
  46.8 6.4 %reshape_reshape.3 = bf16[2,6,3,12,2,16,64]{6,5,4,3,2,1,0:T(8,128)(2,1)} reshape(bf16[432,2048]{1,0:T(8,128)(2,1)} %fusion.17) | data formatting | bytes 3538944 | tf_op jit(solution)/shard_map/reshape;reshape | solution.py:57
  58.4 4.1 %copy.81 = bf16[6,72,1,16,64]{1,4,3,0,2:T(8,128)(2,1)} copy(bf16[6,72,1,16,64]{4,3,2,1,0:T(8,128)(2,1)} %get-tuple-element.18) | data formatting | bytes 1769472
  62.4 4.0 %copy.82 = bf16[6,72,1,16,64]{1,4,3,0,2:T(8,128)(2,1)} copy(bf16[6,72,1,16,64]{4,3,2,1,0:T(8,128)(2,1)} %get-tuple-element.19) | data formatting | bytes 1769472
  73.3 4.0 %copy.68 = bf16[6,72,16,64]{3,2,1,0:T(8,128)(2,1)} copy(bf16[6,72,16,64]{1,3,2,0:T(8,128)(2,1)} %fusion.36) | data formatting | bytes 1769472 | tf_op jit(solution)/shard_map/whqk,wkhd->wqhd/transpose | solution.py:76
  77.3 3.9 %reshape.100 = bf16[2,3,6,12,1024]{4,3,2,1,0:T(8,128)(2,1)} reshape(bf16[6,72,16,64]{3,2,1,0:T(8,128)(2,1)} %copy.68) | data formatting | bytes 1769472 | tf_op jit(solution)/shard_map/reshape | solution.py:78
  88.0 3.8 %collective-permute-start.12 = (bf16[5,64,320]{1,2,0:T(8,128)(2,1)S(1)}, bf16[5,64,320]{1,2,0:T(8,128)(2,1)S(1)}, u32[]{:S(2)}, u32[]{:S(2)}) collective-permute-start(bf16[5,64,320]{1,2,0:T(8,128)(2,1)S(1)} %copy.70), channel_id=1, source_target_pairs={{0,120},{8,0},{16,8},{24,16},{32,24},{40,32},{48,40},{56,48},{64,5... | collective-permute-start | bytes 614408 | tf_op jit(solution)/shard_map/ppermute | solution.py:22
  91.8 10.2 %collective-permute-done.4 = bf16[5,64,320]{1,2,0:T(8,128)(2,1)S(1)} collective-permute-done((bf16[5,64,320]{1,2,0:T(8,128)(2,1)S(1)}, bf16[5,64,320]{1,2,0:T(8,128)(2,1)S(1)}, u32[]{:S(2)}, u32[]{:S(2)}) %collective-permute-start.4) | collective-permute-done | bytes 204832 | tf_op jit(solution)/shard_map/ppermute | solution.py:19
  102.0 5.3 %collective-permute-start.13 = (bf16[5,64,320]{1,2,0:T(8,128)(2,1)S(1)}, bf16[5,64,320]{1,2,0:T(8,128)(2,1)S(1)}, u32[]{:S(2)}, u32[]{:S(2)}) collective-permute-start(bf16[5,64,320]{1,2,0:T(8,128)(2,1)S(1)} %collective-permute-done.12), channel_id=1, source_target_pairs={{0,120},{8,0},{16,8},{24,16},{32,24},{40,32},{48,40},{56,48},{64,5... | collective-permute-start | bytes 614408 | tf_op jit(solution)/shard_map/ppermute | solution.py:22
  107.3 9.3 %collective-permute-done.5 = bf16[5,64,320]{1,2,0:T(8,128)(2,1)S(1)} collective-permute-done((bf16[5,64,320]{1,2,0:T(8,128)(2,1)S(1)}, bf16[5,64,320]{1,2,0:T(8,128)(2,1)S(1)}, u32[]{:S(2)}, u32[]{:S(2)}) %collective-permute-start.5) | collective-permute-done | bytes 204832 | tf_op jit(solution)/shard_map/ppermute | solution.py:19
  116.6 5.3 %collective-permute-start.14 = (bf16[5,64,320]{1,2,0:T(8,128)(2,1)S(1)}, bf16[5,64,320]{1,2,0:T(8,128)(2,1)S(1)}, u32[]{:S(2)}, u32[]{:S(2)}) collective-permute-start(bf16[5,64,320]{1,2,0:T(8,128)(2,1)S(1)} %collective-permute-done.13), channel_id=1, source_target_pairs={{0,120},{8,0},{16,8},{24,16},{32,24},{40,32},{48,40},{56,48},{64,5... | collective-permute-start | bytes 614408 | tf_op jit(solution)/shard_map/ppermute | solution.py:22
  122.0 8.4 %collective-permute-done.6 = bf16[5,64,320]{1,2,0:T(8,128)(2,1)S(1)} collective-permute-done((bf16[5,64,320]{1,2,0:T(8,128)(2,1)S(1)}, bf16[5,64,320]{1,2,0:T(8,128)(2,1)S(1)}, u32[]{:S(2)}, u32[]{:S(2)}) %collective-permute-start.6) | collective-permute-done | bytes 204832 | tf_op jit(solution)/shard_map/ppermute | solution.py:19
  130.4 5.3 %collective-permute-start.15 = (bf16[5,64,320]{1,2,0:T(8,128)(2,1)S(1)}, bf16[5,64,320]{1,2,0:T(8,128)(2,1)}, u32[]{:S(2)}, u32[]{:S(2)}) collective-permute-start(bf16[5,64,320]{1,2,0:T(8,128)(2,1)S(1)} %collective-permute-done.14), channel_id=1, source_target_pairs={{0,120},{8,0},{16,8},{24,16},{32,24},{40,32},{48,40},{56,48},{64,5... | collective-permute-start | bytes 614408 | tf_op jit(solution)/shard_map/ppermute | solution.py:22
  135.8 7.5 %collective-permute-done.7 = bf16[5,64,320]{1,2,0:T(8,128)(2,1)S(1)} collective-permute-done((bf16[5,64,320]{1,2,0:T(8,128)(2,1)S(1)}, bf16[5,64,320]{1,2,0:T(8,128)(2,1)S(1)}, u32[]{:S(2)}, u32[]{:S(2)}) %collective-permute-start.7) | collective-permute-done | bytes 204832 | tf_op jit(solution)/shard_map/ppermute | solution.py:19
  143.3 5.3 %collective-permute-start.16 = (bf16[5,64,320]{1,2,0:T(8,128)(2,1)}, bf16[5,64,320]{1,2,0:T(8,128)(2,1)}, u32[]{:S(2)}, u32[]{:S(2)}) collective-permute-start(bf16[5,64,320]{1,2,0:T(8,128)(2,1)} %collective-permute-done.15), channel_id=1, source_target_pairs={{0,120},{8,0},{16,8},{24,16},{32,24},{40,32},{48,40},{56,48},{64,5... | collective-permute-start | bytes 614408 | tf_op jit(solution)/shard_map/ppermute | solution.py:22
  148.6 6.7 %collective-permute-done.8 = bf16[5,64,320]{1,2,0:T(8,128)(2,1)} collective-permute-done((bf16[5,64,320]{1,2,0:T(8,128)(2,1)S(1)}, bf16[5,64,320]{1,2,0:T(8,128)(2,1)}, u32[]{:S(2)}, u32[]{:S(2)}) %collective-permute-start.8) | collective-permute-done | bytes 204832 | tf_op jit(solution)/shard_map/ppermute | solution.py:19
  155.4 5.3 %collective-permute-start.17 = (bf16[5,64,320]{1,2,0:T(8,128)(2,1)}, bf16[5,64,320]{1,2,0:T(8,128)(2,1)S(1)}, u32[]{:S(2)}, u32[]{:S(2)}) collective-permute-start(bf16[5,64,320]{1,2,0:T(8,128)(2,1)} %collective-permute-done.16), channel_id=1, source_target_pairs={{0,120},{8,0},{16,8},{24,16},{32,24},{40,32},{48,40},{56,48},{64,5... | collective-permute-start | bytes 614408 | tf_op jit(solution)/shard_map/ppermute | solution.py:22
  160.7 6.2 %collective-permute-done.9 = bf16[5,64,320]{1,2,0:T(8,128)(2,1)} collective-permute-done((bf16[5,64,320]{1,2,0:T(8,128)(2,1)}, bf16[5,64,320]{1,2,0:T(8,128)(2,1)}, u32[]{:S(2)}, u32[]{:S(2)}) %collective-permute-start.9) | collective-permute-done | bytes 204832 | tf_op jit(solution)/shard_map/ppermute | solution.py:19
  167.8 5.3 %collective-permute-start.18 = (bf16[5,64,320]{1,2,0:T(8,128)(2,1)S(1)}, bf16[5,64,320]{1,2,0:T(8,128)(2,1)S(1)}, u32[]{:S(2)}, u32[]{:S(2)}) collective-permute-start(bf16[5,64,320]{1,2,0:T(8,128)(2,1)S(1)} %collective-permute-done.17), channel_id=1, source_target_pairs={{0,120},{8,0},{16,8},{24,16},{32,24},{40,32},{48,40},{56,48},{64,5... | collective-permute-start | bytes 614408 | tf_op jit(solution)/shard_map/ppermute | solution.py:22
  173.2 5.3 %collective-permute-done.10 = bf16[5,64,320]{1,2,0:T(8,128)(2,1)S(1)} collective-permute-done((bf16[5,64,320]{1,2,0:T(8,128)(2,1)}, bf16[5,64,320]{1,2,0:T(8,128)(2,1)S(1)}, u32[]{:S(2)}, u32[]{:S(2)}) %collective-permute-start.10) | collective-permute-done | bytes 204832 | tf_op jit(solution)/shard_map/ppermute | solution.py:19
  179.9 9.9 %collective-permute-done.11 = bf16[5,64,320]{1,2,0:T(8,128)(2,1)} collective-permute-done((bf16[5,64,320]{1,2,0:T(8,128)(2,1)S(1)}, bf16[5,64,320]{1,2,0:T(8,128)(2,1)}, u32[]{:S(2)}, u32[]{:S(2)}) %collective-permute-start.11) | collective-permute-done | bytes 204832 | tf_op jit(solution)/shard_map/ppermute | solution.py:19
  189.8 15.2 %concatenate.14 = bf16[5,2048,320]{1,2,0:T(8,128)(2,1)} concatenate(bf16[5,64,320]{1,2,0:T(8,128)(2,1)} %collective-permute-done.11, bf16[5,64,320]{1,2,0:T(8,128)(2,1)} %copy-done.6, bf16[5,64,320]{1,2,0:T(8,128)(2,1)} %collective-permute-done.9, bf16[5,64,320]{1,2,0:T(8,128)(2,1)} %collective-permute-done.8, bf16[5,64,320]{1,2,0:T(8,128)(2,1)S(1)} %collective-permute-done.7, ...), dimensions={1} | concatenate | bytes 13107200 | tf_op jit(solution)/shard_map/jit(_roll_dynamic)/concatenate | solution.py:26
  208.6 10.9 %multiply_convert_fusion = bf16[5,6,192,320]{3,2,1,0:T(8,128)(2,1)S(1)} fusion(bf16[5,6,192,320]{3,2,1,0:T(8,128)(2,1)} %param.18, f32[5,192]{1,0:T(8,128)S(1)} %fusion.54, bf16[5,2048,320]{1,2,0:T(8,128)(2,1)S(1)} %copy-done.2, s32[]{:T(128)S(6)} %select_n.32, f32[5,1024]{1,0:T(8,128)S(1)} %copy-done.12, f32[5,1024]{1,0:T(8,128)S(1)} %copy-done.11, ...), kind=kOutput, calls=%fused_computation.11 | convolution fusion | flops 3799941120 | bytes 15441924 | tf_op jit(solution)/shard_map/krnd,kdo->krno/dot_general | solution.py:89
  219.5 7.3 %multiply_reduce_fusion = bf16[6,192,1024]{2,1,0:T(8,128)(2,1)S(1)} fusion(f32[5,1024]{1,0:T(8,128)S(1)} %copy-done.11, bf16[5,6,192,320]{3,2,1,0:T(8,128)(2,1)S(1)} %multiply_convert_fusion, bf16[5,2048,320]{1,2,0:T(8,128)(2,1)S(1)} %copy-done.2, s32[]{:T(128)S(6)} %select_n.32), kind=kOutput, calls=%fused_computation.1 | convolution fusion | flops 3785490432 | bytes 10092548 | tf_op jit(solution)/shard_map/krno,kdo->krnd/dot_general | solution.py:93
  228.6 9.3 %fusion.12 = bf16[1024,5,320]{0,2,1:T(8,128)(2,1)} fusion(bf16[5,6,192,320]{3,2,1,0:T(8,128)(2,1)} %copy-done.16, f32[5,1024]{1,0:T(8,128)S(1)} %copy-done.12, f32[5,1024]{1,0:T(8,128)S(1)} %copy-done.11, f32[6,192,1024]{2,1,0:T(8,128)} %copy-done.3), kind=kOutput, calls=%fused_computation.19 | convolution fusion | flops 3795845120 | bytes 11722752 | tf_op jit(solution)/shard_map/krnd,krno->dko/dot_general | solution.py:95
  237.9 8.2 %copy.74 = bf16[1024,5,320]{2,1,0:T(8,128)(2,1)} copy(bf16[1024,5,320]{0,2,1:T(8,128)(2,1)} %fusion.12) | data formatting | bytes 6553600 | tf_op jit(solution)/shard_map/convert_element_type | solution.py:167
  246.2 15.6 %reduce-scatter.7.cloned.1.call-done = bf16[24,6144]{1,0:T(8,128)(2,1)} async-done(((bf16[192,6144]{1,0:T(8,128)(2,1)}), bf16[24,6144]{1,0:T(8,128)(2,1)}) %reduce-scatter.7.cloned.1.call-update) | async-done | bytes 294928
  264.0 81.1 %reduce-scatter.5.cloned.1.call-done = bf16[64,5,320]{2,1,0:T(8,128)(2,1)} async-done(((bf16[1024,5,320]{2,1,0:T(8,128)(2,1)}), bf16[64,5,320]{2,1,0:T(8,128)(2,1)}) %reduce-scatter.5.cloned.1.call-update) | async-done | bytes 204816 | tf_op jit(solution)/shard_map/reduce_scatter | solution.py:166
  (100 shorter events, 51.5 us)
Async XLA Ops:
  7.2 76.6 %copy-start = (bf16[1024,1024]{1,0:T(8,128)(2,1)S(1)}, bf16[1024,1024]{1,0:T(8,128)(2,1)}, u32[]{:S(2)}) copy-start(bf16[1024,1024]{1,0:T(8,128)(2,1)} %param.14) | copy-start | bytes 6291460
  7.2 197.9 %all-gather.2.cloned.1.call-start = ((), (), s32[]{:S(2)}) async-start(), calls=%async_computation.2 | async-start | bytes 2654208 | tf_op jit(solution)/shard_map/all_gather | solution.py:151
  8.4 6.7 %collective-permute-start = (bf16[3,24,1024]{2,1,0:T(8,128)(2,1)S(1)}, bf16[3,24,1024]{2,1,0:T(8,128)(2,1)S(1)}, u32[]{:S(2)}, u32[]{:S(2)}) collective-permute-start(bf16[3,24,1024]{2,1,0:T(8,128)(2,1)S(1)} %get-tuple-element.25), channel_id=1, source_target_pairs={{0,8},{8,16},{16,24},{24,32},{32,40},{40,48},{48,56},{56,64},{64,7... | collective-permute-start | bytes 442376 | tf_op jit(solution)/shard_map/ppermute | solution.py:36
  12.0 7.2 %collective-permute-start.1 = (bf16[3,24,1024]{2,1,0:T(8,128)(2,1)S(1)}, bf16[3,24,1024]{2,1,0:T(8,128)(2,1)S(1)}, u32[]{:S(2)}, u32[]{:S(2)}) collective-permute-start(bf16[3,24,1024]{2,1,0:T(8,128)(2,1)S(1)} %get-tuple-element.24), channel_id=1, source_target_pairs={{8,0},{16,8},{24,16},{32,24},{40,32},{48,40},{56,48},{64,56},{72,6... | collective-permute-start | bytes 442376 | tf_op jit(solution)/shard_map/ppermute | solution.py:37
  19.2 6.3 %collective-permute-start.2 = (bf16[12,6,1024]{2,1,0:T(8,128)(2,1)S(1)}, bf16[12,6,1024]{2,1,0:T(8,128)(2,1)S(1)}, u32[]{:S(2)}, u32[]{:S(2)}) collective-permute-start(bf16[12,6,1024]{2,1,0:T(8,128)(2,1)S(1)} %get-tuple-element.22), channel_id=1, source_target_pairs={{0,1},{1,2},{2,3},{3,4},{4,5},{5,6},{6,7},{7,0},{8,9},{9,10},{10,1... | collective-permute-start | bytes 442376 | tf_op jit(solution)/shard_map/ppermute | solution.py:36
  19.3 6.3 %collective-permute-start.3 = (bf16[12,6,1024]{2,1,0:T(8,128)(2,1)S(1)}, bf16[12,6,1024]{2,1,0:T(8,128)(2,1)S(1)}, u32[]{:S(2)}, u32[]{:S(2)}) collective-permute-start(bf16[12,6,1024]{2,1,0:T(8,128)(2,1)S(1)} %get-tuple-element.23), channel_id=1, source_target_pairs={{1,0},{2,1},{3,2},{4,3},{5,4},{6,5},{7,6},{0,7},{9,8},{10,9},{11,1... | collective-permute-start | bytes 442376 | tf_op jit(solution)/shard_map/ppermute | solution.py:37
  27.9 4.5 %copy-start.10 = (f32[1024]{0:T(1024)S(1)}, f32[1024]{0:T(1024)}, u32[]{:S(2)}) copy-start(f32[1024]{0:T(1024)} %param.12) | copy-start | bytes 12292
  82.6 3.6 %copy-start.9 = (bf16[5,64,320]{2,1,0:T(8,128)(2,1)S(1)}, bf16[5,64,320]{2,1,0:T(8,128)(2,1)}, u32[]{:S(2)}) copy-start(bf16[5,64,320]{2,1,0:T(8,128)(2,1)} %param.17) | copy-start | bytes 614404
  82.6 84.4 %copy-start.13 = (s32[4]{0:T(128)S(1)}, s32[4]{0:T(128)}, u32[]{:S(2)}) copy-start(s32[4]{0:T(128)} %param.19) | copy-start | bytes 52
  82.6 84.4 %copy-start.14 = (s32[1,8]{1,0:T(1,128)S(1)}, s32[1,8]{1,0:T(1,128)}, u32[]{:S(2)}) copy-start(s32[1,8]{1,0:T(1,128)} %param.20) | copy-start | bytes 100
  82.6 95.8 %copy-start.15 = (s32[5]{0:T(128)S(1)}, s32[5]{0:T(128)}, u32[]{:S(2)}) copy-start(s32[5]{0:T(128)} %param.21) | copy-start | bytes 64
  86.1 175.6 %reduce-scatter.7.cloned.1.call-start = ((), (), s32[]{:S(2)}) async-start(), calls=%async_computation.4 | async-start | bytes 2654208
  86.4 15.6 %collective-permute-start.4 = (bf16[5,64,320]{1,2,0:T(8,128)(2,1)S(1)}, bf16[5,64,320]{1,2,0:T(8,128)(2,1)S(1)}, u32[]{:S(2)}, u32[]{:S(2)}) collective-permute-start(bf16[5,64,320]{1,2,0:T(8,128)(2,1)S(1)} %copy.70), channel_id=1, source_target_pairs={{0,8},{8,16},{16,24},{24,32},{32,40},{40,48},{48,56},{56,64},{64,7... | collective-permute-start | bytes 614408 | tf_op jit(solution)/shard_map/ppermute | solution.py:19
  88.0 13.9 %collective-permute-start.12 = (bf16[5,64,320]{1,2,0:T(8,128)(2,1)S(1)}, bf16[5,64,320]{1,2,0:T(8,128)(2,1)S(1)}, u32[]{:S(2)}, u32[]{:S(2)}) collective-permute-start(bf16[5,64,320]{1,2,0:T(8,128)(2,1)S(1)} %copy.70), channel_id=1, source_target_pairs={{0,120},{8,0},{16,8},{24,16},{32,24},{40,32},{48,40},{56,48},{64,5... | collective-permute-start | bytes 614408 | tf_op jit(solution)/shard_map/ppermute | solution.py:22
  102.0 14.7 %collective-permute-start.5 = (bf16[5,64,320]{1,2,0:T(8,128)(2,1)S(1)}, bf16[5,64,320]{1,2,0:T(8,128)(2,1)S(1)}, u32[]{:S(2)}, u32[]{:S(2)}) collective-permute-start(bf16[5,64,320]{1,2,0:T(8,128)(2,1)S(1)} %collective-permute-done.4), channel_id=1, source_target_pairs={{0,8},{8,16},{16,24},{24,32},{32,40},{40,48},{48,56},{56,64},{64,7... | collective-permute-start | bytes 614408 | tf_op jit(solution)/shard_map/ppermute | solution.py:19
  102.0 14.7 %collective-permute-start.13 = (bf16[5,64,320]{1,2,0:T(8,128)(2,1)S(1)}, bf16[5,64,320]{1,2,0:T(8,128)(2,1)S(1)}, u32[]{:S(2)}, u32[]{:S(2)}) collective-permute-start(bf16[5,64,320]{1,2,0:T(8,128)(2,1)S(1)} %collective-permute-done.12), channel_id=1, source_target_pairs={{0,120},{8,0},{16,8},{24,16},{32,24},{40,32},{48,40},{56,48},{64,5... | collective-permute-start | bytes 614408 | tf_op jit(solution)/shard_map/ppermute | solution.py:22
  116.6 13.8 %collective-permute-start.6 = (bf16[5,64,320]{1,2,0:T(8,128)(2,1)S(1)}, bf16[5,64,320]{1,2,0:T(8,128)(2,1)S(1)}, u32[]{:S(2)}, u32[]{:S(2)}) collective-permute-start(bf16[5,64,320]{1,2,0:T(8,128)(2,1)S(1)} %collective-permute-done.5), channel_id=1, source_target_pairs={{0,8},{8,16},{16,24},{24,32},{32,40},{40,48},{48,56},{56,64},{64,7... | collective-permute-start | bytes 614408 | tf_op jit(solution)/shard_map/ppermute | solution.py:19
  116.6 13.8 %collective-permute-start.14 = (bf16[5,64,320]{1,2,0:T(8,128)(2,1)S(1)}, bf16[5,64,320]{1,2,0:T(8,128)(2,1)S(1)}, u32[]{:S(2)}, u32[]{:S(2)}) collective-permute-start(bf16[5,64,320]{1,2,0:T(8,128)(2,1)S(1)} %collective-permute-done.13), channel_id=1, source_target_pairs={{0,120},{8,0},{16,8},{24,16},{32,24},{40,32},{48,40},{56,48},{64,5... | collective-permute-start | bytes 614408 | tf_op jit(solution)/shard_map/ppermute | solution.py:22
  130.4 12.9 %collective-permute-start.7 = (bf16[5,64,320]{1,2,0:T(8,128)(2,1)S(1)}, bf16[5,64,320]{1,2,0:T(8,128)(2,1)S(1)}, u32[]{:S(2)}, u32[]{:S(2)}) collective-permute-start(bf16[5,64,320]{1,2,0:T(8,128)(2,1)S(1)} %collective-permute-done.6), channel_id=1, source_target_pairs={{0,8},{8,16},{16,24},{24,32},{32,40},{40,48},{48,56},{56,64},{64,7... | collective-permute-start | bytes 614408 | tf_op jit(solution)/shard_map/ppermute | solution.py:19
  130.4 12.9 %collective-permute-start.15 = (bf16[5,64,320]{1,2,0:T(8,128)(2,1)S(1)}, bf16[5,64,320]{1,2,0:T(8,128)(2,1)}, u32[]{:S(2)}, u32[]{:S(2)}) collective-permute-start(bf16[5,64,320]{1,2,0:T(8,128)(2,1)S(1)} %collective-permute-done.14), channel_id=1, source_target_pairs={{0,120},{8,0},{16,8},{24,16},{32,24},{40,32},{48,40},{56,48},{64,5... | collective-permute-start | bytes 614408 | tf_op jit(solution)/shard_map/ppermute | solution.py:22
  143.3 12.1 %collective-permute-start.8 = (bf16[5,64,320]{1,2,0:T(8,128)(2,1)S(1)}, bf16[5,64,320]{1,2,0:T(8,128)(2,1)}, u32[]{:S(2)}, u32[]{:S(2)}) collective-permute-start(bf16[5,64,320]{1,2,0:T(8,128)(2,1)S(1)} %collective-permute-done.7), channel_id=1, source_target_pairs={{0,8},{8,16},{16,24},{24,32},{32,40},{40,48},{48,56},{56,64},{64,7... | collective-permute-start | bytes 614408 | tf_op jit(solution)/shard_map/ppermute | solution.py:19
  143.3 12.1 %collective-permute-start.16 = (bf16[5,64,320]{1,2,0:T(8,128)(2,1)}, bf16[5,64,320]{1,2,0:T(8,128)(2,1)}, u32[]{:S(2)}, u32[]{:S(2)}) collective-permute-start(bf16[5,64,320]{1,2,0:T(8,128)(2,1)} %collective-permute-done.15), channel_id=1, source_target_pairs={{0,120},{8,0},{16,8},{24,16},{32,24},{40,32},{48,40},{56,48},{64,5... | collective-permute-start | bytes 614408 | tf_op jit(solution)/shard_map/ppermute | solution.py:22
  155.4 11.6 %collective-permute-start.9 = (bf16[5,64,320]{1,2,0:T(8,128)(2,1)}, bf16[5,64,320]{1,2,0:T(8,128)(2,1)}, u32[]{:S(2)}, u32[]{:S(2)}) collective-permute-start(bf16[5,64,320]{1,2,0:T(8,128)(2,1)} %collective-permute-done.8), channel_id=1, source_target_pairs={{0,8},{8,16},{16,24},{24,32},{32,40},{40,48},{48,56},{56,64},{64,7... | collective-permute-start | bytes 614408 | tf_op jit(solution)/shard_map/ppermute | solution.py:19
  155.4 11.7 %collective-permute-start.17 = (bf16[5,64,320]{1,2,0:T(8,128)(2,1)}, bf16[5,64,320]{1,2,0:T(8,128)(2,1)S(1)}, u32[]{:S(2)}, u32[]{:S(2)}) collective-permute-start(bf16[5,64,320]{1,2,0:T(8,128)(2,1)} %collective-permute-done.16), channel_id=1, source_target_pairs={{0,120},{8,0},{16,8},{24,16},{32,24},{40,32},{48,40},{56,48},{64,5... | collective-permute-start | bytes 614408 | tf_op jit(solution)/shard_map/ppermute | solution.py:22
  166.9 11.5 %collective-permute-start.10 = (bf16[5,64,320]{1,2,0:T(8,128)(2,1)}, bf16[5,64,320]{1,2,0:T(8,128)(2,1)S(1)}, u32[]{:S(2)}, u32[]{:S(2)}) collective-permute-start(bf16[5,64,320]{1,2,0:T(8,128)(2,1)} %collective-permute-done.9), channel_id=1, source_target_pairs={{0,8},{8,16},{16,24},{24,32},{32,40},{40,48},{48,56},{56,64},{64,7... | collective-permute-start | bytes 614408 | tf_op jit(solution)/shard_map/ppermute | solution.py:19
  167.8 10.9 %collective-permute-start.18 = (bf16[5,64,320]{1,2,0:T(8,128)(2,1)S(1)}, bf16[5,64,320]{1,2,0:T(8,128)(2,1)S(1)}, u32[]{:S(2)}, u32[]{:S(2)}) collective-permute-start(bf16[5,64,320]{1,2,0:T(8,128)(2,1)S(1)} %collective-permute-done.17), channel_id=1, source_target_pairs={{0,120},{8,0},{16,8},{24,16},{32,24},{40,32},{48,40},{56,48},{64,5... | collective-permute-start | bytes 614408 | tf_op jit(solution)/shard_map/ppermute | solution.py:22
  178.4 11.4 %collective-permute-start.11 = (bf16[5,64,320]{1,2,0:T(8,128)(2,1)S(1)}, bf16[5,64,320]{1,2,0:T(8,128)(2,1)}, u32[]{:S(2)}, u32[]{:S(2)}) collective-permute-start(bf16[5,64,320]{1,2,0:T(8,128)(2,1)S(1)} %collective-permute-done.10), channel_id=1, source_target_pairs={{0,8},{8,16},{16,24},{24,32},{32,40},{40,48},{48,56},{56,64},{64,7... | collective-permute-start | bytes 614408 | tf_op jit(solution)/shard_map/ppermute | solution.py:19
  205.1 3.6 %copy-start.2 = (bf16[5,2048,320]{1,2,0:T(8,128)(2,1)S(1)}, bf16[5,2048,320]{1,2,0:T(8,128)(2,1)}, u32[]{:S(2)}) copy-start(bf16[5,2048,320]{1,2,0:T(8,128)(2,1)} %concatenate.14) | copy-start | bytes 19660804
  208.6 10.9 %copy-start.3 = (f32[6,192,1024]{2,1,0:T(8,128)}, f32[6,192,1024]{2,1,0:T(8,128)S(1)}, u32[]{:S(2)}) copy-start(f32[6,192,1024]{2,1,0:T(8,128)S(1)} %convert_element_type.67) | copy-start | bytes 14155780
  219.5 7.4 %copy-start.16 = (bf16[5,6,192,320]{3,2,1,0:T(8,128)(2,1)}, bf16[5,6,192,320]{3,2,1,0:T(8,128)(2,1)S(1)}, u32[]{:S(2)}) copy-start(bf16[5,6,192,320]{3,2,1,0:T(8,128)(2,1)S(1)} %multiply_convert_fusion) | copy-start | bytes 11059204
  228.6 116.4 %reduce-scatter.5.cloned.1.call-start = ((), (), s32[]{:S(2)}) async-start(), calls=%async_computation.3 | async-start | bytes 6684672 | tf_op jit(solution)/shard_map/reduce_scatter | solution.py:166
  246.1 100.8 %copy-start.1 = (bf16[1024,1024]{1,0:T(8,128)(2,1)S(1)}, bf16[1024,1024]{1,0:T(8,128)(2,1)}, u32[]{:S(2)}) copy-start(bf16[1024,1024]{1,0:T(8,128)(2,1)} %param.14) | copy-start | bytes 6291460
  (7 other events, 12.2 us)
Sparse Core Ops, SparseCore 0:
  86.2 29.4 all-gather.1
  228.7 32.9 reduce-scatter.6
  265.2 79.8 reduce-scatter.4
